TPU v7x, 256 devices: a whole 4x4x8 slice. The times are simulated.
256 devices in a mesh: grp: 4 (over z_lo), row: 4 (over x), col: 16 (over y, z_hi, core).
Axes of the slice: x: 4, y: 4, z: 8 (z_hi: 2, z_lo: 4; z = z_hi * 4 + z_lo), core: 2. Of those that a mesh axis runs over, the one named last changes fastest.
Arguments:
- outer_params: float32 [8192, 1024], P('col', 'row'), may hold values from -0.0625 to 0.0625
- first_moment: float32 [4, 8192, 1024], P('grp', 'col', 'row'), may hold values from -0.12 to 0.12
- second_moment: float32 [4, 8192, 1024], P('grp', 'col', 'row'), may hold values from 0.0001 to 0.01
- outer_moment: float32 [8192, 1024], P('col', 'row'), may hold values from -0.06 to 0.06
- activations: bfloat16 [4, 3, 2048, 8192], P('grp', None, 'row', 'col'), may hold values from -6 to 6
- targets: bfloat16 [4, 3, 2048, 1024], P('grp', None, 'col', 'row'), may hold values from -6 to 6
Outputs:
- new_params: float32 [8192, 1024], P('col', 'row')
- new_moment: float32 [8192, 1024], P('col', 'row')
All inputs are finite; a program needn't handle non-finite values.
Results may differ from a plain program's by a relative error of at most 0.0054.
Values may be sent and summed in bfloat16 or wider, within the bound.
A program may use at most 64 MiB of HBM per device.

v0:
```python
import jax
import jax.numpy as jnp
from jax import lax
from jax.sharding import Mesh
from jax.sharding import PartitionSpec as P

TOKENS = 2048
STEPS = 3
SLOW_STEPS = 1
PRIOR = 100
COL = ("col_0", "col_1", "col_2")
beta_first = 0.9
beta_second = 0.95
inner_rate = 0.01
decay_rate = 0.1
epsilon_value = 1e-08
outer_rate = 0.7
momentum_coef = 0.9


def split_up(shard, dim, count):
    before, after = (shard.shape[:dim], shard.shape[dim + 1 :])
    return jnp.moveaxis(shard.reshape(*before, count, -1, *after), dim, 0)


def summed_on_arrival(shard, axis, dim):
    count = lax.axis_size(axis)
    parts = lax.all_to_all(split_up(shard, dim, count), axis, 0, 0, tiled=True)
    return jnp.sum(parts, axis=0)


def sum_in_two_steps(shard, axes, dim):
    far, near = axes
    own = summed_on_arrival(split_up(shard, dim, lax.axis_size(far)), near, dim + 1)
    return jnp.sum(lax.all_to_all(own, far, 0, 0, tiled=True), axis=0)


def filled_up(lines, count):
    spare = -lines.shape[0] % count
    if not spare:
        return lines
    return jnp.concatenate([lines, jnp.zeros((spare, *lines.shape[1:]), lines.dtype)])


def sent_to_all(shard, axis):
    copies = jnp.broadcast_to(shard, (lax.axis_size(axis), *shard.shape))
    return lax.all_to_all(copies, axis, split_axis=0, concat_axis=0, tiled=True)


def in_order(parts, dim):
    shape = list(parts.shape[1:])
    shape[dim] *= parts.shape[0]
    return jnp.moveaxis(parts, 0, dim).reshape(shape)


def whole_of(shard, axes, dim):
    far, near = axes
    parts = sent_to_all(sent_to_all(shard, far), near)
    return in_order(parts.swapaxes(0, 1).reshape(-1, *shard.shape), dim)


def total_of(shard, axes):
    lines = shard.reshape(-1, shard.shape[-1])
    own = sum_in_two_steps(
        filled_up(lines, lax.axis_size(axes[0]) * lax.axis_size(axes[1])), axes, 0
    )
    whole = whole_of(own, axes, 0)
    return whole[: len(lines)].reshape(shard.shape)


def over_copies(shard, axis):
    everything = sent_to_all(shard, axis)
    return jnp.sum(everything, axis=0)


def local(outer_params, first_moment, second_moment, outer_moment, activations, targets):
    unit = lax.axis_index("grp")
    gathered = lax.all_gather(activations[0], "row", axis=1, tiled=True)
    wanted_all = targets[0]
    wanted_all = lax.all_gather(wanted_all, COL, axis=1, tiled=True)
    first = first_moment[0]
    second = second_moment[0]
    params = outer_params
    for inner_step in range(STEPS):
        inputs = gathered[inner_step]
        partial_value = jnp.dot(
            inputs, params.astype(jnp.bfloat16), preferred_element_type=jnp.float32
        )
        output = total_of(partial_value, (("col_0", "col_1"), "col_2"))
        residual = (output - wanted_all[inner_step].astype(jnp.float32)).astype(jnp.bfloat16)
        gradient = (
            lax.dot_general(
                inputs, residual, (((0,), (0,)), ((), ())), preferred_element_type=jnp.float32
            )
            / TOKENS
        )
        first_next = beta_first * first + (1.0 - beta_first) * gradient
        second_next = beta_second * second + (1.0 - beta_second) * gradient * gradient
        power = PRIOR + inner_step + 1
        corrected = (
            first_next
            / (1.0 - beta_first**power)
            / (jnp.sqrt(second_next / (1.0 - beta_second**power)) + epsilon_value)
        )
        params_next = params - inner_rate * (corrected + decay_rate * params)
        active = jnp.logical_or(unit < 3, inner_step < SLOW_STEPS)
        params = jnp.where(active, params_next, params)
        first = jnp.where(active, first_next, first)
        second = jnp.where(active, second_next, second)
    total_steps = float(3 * STEPS + SLOW_STEPS)
    weight = jnp.where(unit < 3, float(STEPS), float(SLOW_STEPS)) / total_steps
    term = weight * (outer_params - params)
    pseudo = over_copies(term, "grp")
    new_moment = momentum_coef * outer_moment + pseudo
    new_params = outer_params - outer_rate * (pseudo + momentum_coef * new_moment)
    return (new_params, new_moment)


def solution(mesh):
    finer = Mesh(
        mesh.devices.reshape(mesh.shape["grp"], mesh.shape["row"], 4, 2, 2),
        ("grp", "row", "col_0", "col_1", "col_2"),
    )
    placed = (
        P(COL, "row"),
        P("grp", COL, "row"),
        P("grp", COL, "row"),
        P(COL, "row"),
        P("grp", None, "row", COL),
        P("grp", None, COL, "row"),
    )
    return jax.shard_map(
        local,
        mesh=finer,
        in_specs=placed,
        out_specs=(P(COL, "row"), P(COL, "row")),
        check_vma=False,
    )
```

profile of v0, /device:TPU:1, one launch (start us, length us, event | category | flops | bytes accessed | tf_op | source)
XLA Modules:
  0.0 409.2 jit_solution(15068283860982565642)
XLA Ops:
  8.7 73.2 %all-gather.5.cloned.1.call-done = bf16[1,3,2048,512]{3,2,1,0:T(8,128)(2,1)} async-done(((bf16[1,3,512,512]{3,2,1,0:T(8,128)(2,1)}), bf16[1,3,2048,512]{3,2,1,0:T(8,128)(2,1)}) %all-gather.5.cloned.1.call-update) | async-done | bytes 6291472 | tf_op jit(solution)/shard_map/all_gather | solution.py:78
  81.8 1.6 slice-done.6
  84.3 5.8 %all_to_all.65 = f32[2,8,128,256]{3,2,1,0:T(8,128)S(1)} all-to-all(f32[2,8,128,256]{3,2,1,0:T(8,128)S(1)} %copy.76), channel_id=1, replica_groups=mesh['grp'=4,'row'=4,'col_0'=4,'col_1'=2,'col_2'=2] {'col_2'}, dimensions={0} | all-to-all | bytes 4194304 | tf_op jit(solution)/shard_map/all_to_all | solution.py:28
  90.3 35.3 %all_to_all.66 = f32[8,128,256]{2,1,0:T(8,128)S(1)} all-to-all(f32[8,128,256]{2,1,0:T(8,128)S(1)} %reduce_sum.63), channel_id=1, replica_groups=mesh['grp'=4,'row'=4,'col_0'=4,'col_1'=2,'col_2'=2] {'col_0','col_1'}, dimensions={0} | all-to-all | bytes 2097152 | tf_op jit(solution)/shard_map/all_to_all | solution.py:35
  125.7 1.1 broadcast_in_dim.21
  126.8 7.7 %all-to-all-start.2 = ((f32[8,128,256]{2,1,0:T(8,128)}), f32[8,128,256]{2,1,0:T(8,128)S(1)}, u32[]{:S(2)}, u32[]{:S(2)}) async-start(f32[8,128,256]{2,1,0:T(8,128)} %broadcast_in_dim.21), calls=%async_computation.2 | async-start | bytes 2097152 | tf_op jit(solution)/shard_map/all_to_all | solution.py:47
  134.8 1.0 copy.75
  136.0 35.4 %all-gather.7.cloned.1.call-done = bf16[1,3,2048,256]{3,2,1,0:T(8,128)(2,1)} async-done(((bf16[1,3,128,256]{3,2,1,0:T(8,128)(2,1)}), bf16[1,3,2048,256]{3,2,1,0:T(8,128)(2,1)}) %all-gather.7.cloned.1.call-update) | async-done | bytes 3145744 | tf_op jit(solution)/shard_map/all_gather | solution.py:80
  171.4 3.4 fusion.43
  175.0 5.7 %all_to_all.67 = f32[2,8,128,256]{3,2,1,0:T(8,128)S(1)} all-to-all(f32[2,8,128,256]{3,2,1,0:T(8,128)S(1)} %broadcast_in_dim.22), channel_id=1, replica_groups=mesh['grp'=4,'row'=4,'col_0'=4,'col_1'=2,'col_2'=2] {'col_2'}, dimensions={0} | all-to-all | bytes 4194304 | tf_op jit(solution)/shard_map/all_to_all | solution.py:47
  182.7 2.4 convolution_bitcast_fusion.1
  185.2 3.0 reshape_reshape.4
  188.3 5.4 %all_to_all.68 = f32[2,8,128,256]{2,1,3,0:T(8,128)S(1)} all-to-all(f32[2,8,128,256]{2,1,3,0:T(8,128)S(1)} %bitcast.148), channel_id=1, replica_groups=mesh['grp'=4,'row'=4,'col_0'=4,'col_1'=2,'col_2'=2] {'col_2'}, dimensions={0} | all-to-all | bytes 4194304 | tf_op jit(solution)/shard_map/all_to_all | solution.py:28
  194.2 21.3 %all_to_all.69 = f32[8,128,256]{1,2,0:T(8,128)S(1)} all-to-all(f32[8,128,256]{1,2,0:T(8,128)S(1)} %copy.83), channel_id=1, replica_groups=mesh['grp'=4,'row'=4,'col_0'=4,'col_1'=2,'col_2'=2] {'col_0','col_1'}, dimensions={0} | all-to-all | bytes 2097152 | tf_op jit(solution)/shard_map/all_to_all | solution.py:35
  215.7 1.0 broadcast_in_dim.23
  216.7 3.6 all-to-all-start.6
  220.3 24.7 %all-to-all-done.6 = f32[8,128,256]{2,1,0:T(8,128)S(1)} async-done(((f32[8,128,256]{2,1,0:T(8,128)}), f32[8,128,256]{2,1,0:T(8,128)S(1)}, u32[]{:S(2)}, u32[]{:S(2)}) %all-to-all-start.6) | async-done | bytes 1048608 | tf_op jit(solution)/shard_map/all_to_all | solution.py:47
  245.2 6.0 %all_to_all.70 = f32[2,8,128,256]{3,2,1,0:T(8,128)S(1)} all-to-all(f32[2,8,128,256]{3,2,1,0:T(8,128)S(1)} %broadcast_in_dim.24), channel_id=1, replica_groups=mesh['grp'=4,'row'=4,'col_0'=4,'col_1'=2,'col_2'=2] {'col_2'}, dimensions={0} | all-to-all | bytes 4194304 | tf_op jit(solution)/shard_map/all_to_all | solution.py:47
  253.1 2.9 convolution_bitcast_fusion
  256.0 3.0 reshape_reshape.5
  259.2 5.4 %all_to_all.71 = f32[2,8,128,256]{2,1,3,0:T(8,128)S(1)} all-to-all(f32[2,8,128,256]{2,1,3,0:T(8,128)S(1)} %bitcast.149), channel_id=1, replica_groups=mesh['grp'=4,'row'=4,'col_0'=4,'col_1'=2,'col_2'=2] {'col_2'}, dimensions={0} | all-to-all | bytes 4194304 | tf_op jit(solution)/shard_map/all_to_all | solution.py:28
  265.1 25.3 %all_to_all.72 = f32[8,128,256]{1,2,0:T(8,128)S(1)} all-to-all(f32[8,128,256]{1,2,0:T(8,128)S(1)} %copy.89), channel_id=1, replica_groups=mesh['grp'=4,'row'=4,'col_0'=4,'col_1'=2,'col_2'=2] {'col_0','col_1'}, dimensions={0} | all-to-all | bytes 2097152 | tf_op jit(solution)/shard_map/all_to_all | solution.py:35
  290.5 1.0 broadcast_in_dim.25
  291.5 3.6 all-to-all-start.10
  295.1 20.5 %all-to-all-done.10 = f32[8,128,256]{2,1,0:T(8,128)S(1)} async-done(((f32[8,128,256]{2,1,0:T(8,128)}), f32[8,128,256]{2,1,0:T(8,128)S(1)}, u32[]{:S(2)}, u32[]{:S(2)}) %all-to-all-start.10) | async-done | bytes 1048608 | tf_op jit(solution)/shard_map/all_to_all | solution.py:47
  315.8 6.9 %all_to_all.73 = f32[2,8,128,256]{3,2,1,0:T(8,128)S(1)} all-to-all(f32[2,8,128,256]{3,2,1,0:T(8,128)S(1)} %broadcast_in_dim.26), channel_id=1, replica_groups=mesh['grp'=4,'row'=4,'col_0'=4,'col_1'=2,'col_2'=2] {'col_2'}, dimensions={0} | all-to-all | bytes 4194304 | tf_op jit(solution)/shard_map/all_to_all | solution.py:47
  324.4 3.4 fusion.8
  328.0 1.5 broadcast_in_dim.27
  329.5 20.7 %all-to-all-start.12 = ((f32[4,512,256]{2,1,0:T(8,128)}), f32[4,512,256]{2,1,0:T(8,128)S(1)}, u32[]{:S(2)}, u32[]{:S(2)}) async-start(f32[4,512,256]{2,1,0:T(8,128)} %broadcast_in_dim.27), calls=%async_computation.12 | async-start | bytes 4194304 | tf_op jit(solution)/shard_map/all_to_all | solution.py:47
  350.3 1.2 copy.95
  351.5 46.5 %all-to-all-done.12 = f32[4,512,256]{2,1,0:T(8,128)S(1)} async-done(((f32[4,512,256]{2,1,0:T(8,128)}), f32[4,512,256]{2,1,0:T(8,128)S(1)}, u32[]{:S(2)}, u32[]{:S(2)}) %all-to-all-start.12) | async-done | bytes 2097184 | tf_op jit(solution)/shard_map/all_to_all | solution.py:47
  399.0 1.2 copy.97
  (90 shorter events, 13.9 us)
Async XLA Ops:
  7.2 74.7 %all-gather.5.cloned.1.call-start = ((), (), s32[]{:S(2)}) async-start(), calls=%async_computation.13 | async-start | bytes 7864320 | tf_op jit(solution)/shard_map/all_gather | solution.py:78
  7.9 163.5 %all-gather.7.cloned.1.call-start = ((), (), s32[]{:S(2)}) async-start(), calls=%async_computation.14 | async-start | bytes 3342336 | tf_op jit(solution)/shard_map/all_gather | solution.py:80
  8.6 73.2 %copy-start.2 = (f32[512,256]{1,0:T(8,128)S(1)}, f32[512,256]{1,0:T(8,128)}, u32[]{:S(2)}) copy-start(f32[512,256]{1,0:T(8,128)} %param.6) | copy-start | bytes 1572868
  81.8 1.6 slice-start.6
  125.6 8.9 %copy-start.3 = (f32[512,256]{1,0:T(8,128)S(1)}, f32[512,256]{1,0:T(8,128)}, u32[]{:S(2)}) copy-start(f32[512,256]{1,0:T(8,128)} %param.6) | copy-start | bytes 1572868
  125.7 9.1 %copy-start.7 = (f32[1,512,256]{2,1,0:T(8,128)S(1)}, f32[1,512,256]{2,1,0:T(8,128)}, u32[]{:S(2)}) copy-start(f32[1,512,256]{2,1,0:T(8,128)} %param.7) | copy-start | bytes 1572868
  126.8 9.0 %copy-start.8 = (f32[1,512,256]{2,1,0:T(8,128)S(1)}, f32[1,512,256]{2,1,0:T(8,128)}, u32[]{:S(2)}) copy-start(f32[1,512,256]{2,1,0:T(8,128)} %param.8) | copy-start | bytes 1572868
  126.8 47.9 %all-to-all-start.2 = ((f32[8,128,256]{2,1,0:T(8,128)}), f32[8,128,256]{2,1,0:T(8,128)S(1)}, u32[]{:S(2)}, u32[]{:S(2)}) async-start(f32[8,128,256]{2,1,0:T(8,128)} %broadcast_in_dim.21), calls=%async_computation.2 | async-start | bytes 2097152 | tf_op jit(solution)/shard_map/all_to_all | solution.py:47
  134.8 47.1 %copy-start.4 = (f32[512,256]{0,1:T(8,128)}, f32[512,256]{0,1:T(8,128)S(1)}, u32[]{:S(2)}) copy-start(f32[512,256]{0,1:T(8,128)S(1)} %copy.98) | copy-start | bytes 1572868
  136.0 45.9 %copy-start.12 = (f32[1,512,256]{1,2,0:T(8,128)}, f32[1,512,256]{1,2,0:T(8,128)S(1)}, u32[]{:S(2)}) copy-start(f32[1,512,256]{1,2,0:T(8,128)S(1)} %copy.78) | copy-start | bytes 1572868
  174.8 6.3 %slice-start = ((s8[6291456]{0:T(1024)(128)(4,1)}), s8[4194304]{0:T(1024)(128)(4,1)S(1)}, s32[]{:S(2)}) async-start(s8[6291456]{0:T(1024)(128)(4,1)} %bitcast.150), calls=%async_computation.15 | async-start | bytes 8388608
  175.0 6.1 %slice-start.1 = ((s8[6291456]{0:T(1024)(128)(4,1)}), s8[2097152]{0:T(1024)(128)(4,1)S(1)}, s32[]{:S(2)}) async-start(s8[6291456]{0:T(1024)(128)(4,1)} %bitcast.150), calls=%async_computation.16 | async-start | bytes 4194304
  181.1 1.6 copy-start.9
  181.9 0.9 copy-start.15
  216.7 28.3 %all-to-all-start.6 = ((f32[8,128,256]{2,1,0:T(8,128)}), f32[8,128,256]{2,1,0:T(8,128)S(1)}, u32[]{:S(2)}, u32[]{:S(2)}) async-start(f32[8,128,256]{2,1,0:T(8,128)} %broadcast_in_dim.23), calls=%async_computation.6 | async-start | bytes 2097152 | tf_op jit(solution)/shard_map/all_to_all | solution.py:47
  245.0 6.5 %slice-start.2 = ((s8[6291456]{0:T(1024)(128)(4,1)}), s8[4194304]{0:T(1024)(128)(4,1)S(1)}, s32[]{:S(2)}) async-start(s8[6291456]{0:T(1024)(128)(4,1)} %bitcast.152), calls=%async_computation.17 | async-start | bytes 8388608
  245.2 6.0 %copy-start.1 = (bf16[1,1,2048,256]{3,2,1,0:T(8,128)(2,1)S(1)}, bf16[1,1,2048,256]{3,2,1,0:T(8,128)(2,1)}, u32[]{:S(2)}) copy-start(bf16[1,1,2048,256]{3,2,1,0:T(8,128)(2,1)} %get-tuple-element.13) | copy-start | bytes 3145732
  245.2 6.3 %slice-start.3 = ((s8[6291456]{0:T(1024)(128)(4,1)}), s8[2097152]{0:T(1024)(128)(4,1)S(1)}, s32[]{:S(2)}) async-start(s8[6291456]{0:T(1024)(128)(4,1)} %bitcast.152), calls=%async_computation.18 | async-start | bytes 4194304
  251.6 1.6 copy-start.5
  251.6 1.6 copy-start.10
  251.6 1.5 copy-start.13
  251.6 1.5 copy-start.16
  291.5 24.0 %all-to-all-start.10 = ((f32[8,128,256]{2,1,0:T(8,128)}), f32[8,128,256]{2,1,0:T(8,128)S(1)}, u32[]{:S(2)}, u32[]{:S(2)}) async-start(f32[8,128,256]{2,1,0:T(8,128)} %broadcast_in_dim.25), calls=%async_computation.10 | async-start | bytes 2097152 | tf_op jit(solution)/shard_map/all_to_all | solution.py:47
  315.6 7.5 %slice-start.4 = ((s8[6291456]{0:T(1024)(128)(4,1)}), s8[4194304]{0:T(1024)(128)(4,1)S(1)}, s32[]{:S(2)}) async-start(s8[6291456]{0:T(1024)(128)(4,1)} %bitcast.154), calls=%async_computation.19 | async-start | bytes 8388608
  315.8 6.9 %copy-start = (bf16[1,1,2048,256]{3,2,1,0:T(8,128)(2,1)S(1)}, bf16[1,1,2048,256]{3,2,1,0:T(8,128)(2,1)}, u32[]{:S(2)}) copy-start(bf16[1,1,2048,256]{3,2,1,0:T(8,128)(2,1)} %get-tuple-element.14) | copy-start | bytes 3145732
  315.8 7.3 %slice-start.5 = ((s8[6291456]{0:T(1024)(128)(4,1)}), s8[2097152]{0:T(1024)(128)(4,1)S(1)}, s32[]{:S(2)}) async-start(s8[6291456]{0:T(1024)(128)(4,1)} %bitcast.154), calls=%async_computation.20 | async-start | bytes 4194304
  322.7 1.0 copy-start.6
  322.7 1.2 copy-start.11
  322.7 1.4 copy-start.14
  322.7 1.5 copy-start.17
  322.8 1.7 copy-start.19
  329.5 68.5 %all-to-all-start.12 = ((f32[4,512,256]{2,1,0:T(8,128)}), f32[4,512,256]{2,1,0:T(8,128)S(1)}, u32[]{:S(2)}, u32[]{:S(2)}) async-start(f32[4,512,256]{2,1,0:T(8,128)} %broadcast_in_dim.27), calls=%async_computation.12 | async-start | bytes 4194304 | tf_op jit(solution)/shard_map/all_to_all | solution.py:47
  (1 other events, 0.8 us)
Sparse Core Ops, SparseCore 0:
  9.8 71.9 all-gather.4
  84.6 86.7 all-gather.6
where the time goes:
time: 410 us; the launch traced here: 409 us
  waiting for transfers between devices  202 us (49%)
  blocking collectives  117 us (29%)
  starting transfers between devices  35.7 us (9%)
  local copies, waits for them, and re-layouts  26.5 us (6%)
  between operations  14.6 us (4%)
  matrix products  10.9 us (3%)
    all_to_all x4, waiting for transfers between devices, sent_to_all(): return lax.all_to_all(copies, axis, split_axis=0, concat_axis=0, tiled=True)  91.7 us
    all_to_all x3, blocking collectives, sum_in_two_steps(): return jnp.sum(lax.all_to_all(own, far, 0, 0, tiled=True), axis=0)  81.9 us
    all_gather x1, waiting for transfers between devices, local(): gathered = lax.all_gather(activations[0], 'row', axis=1, tiled=True)  73.2 us
    all_to_all x4, starting transfers between devices, sent_to_all(): return lax.all_to_all(copies, axis, split_axis=0, concat_axis=0, tiled=True)  35.6 us
    all_gather x1, waiting for transfers between devices, local(): wanted_all = lax.all_gather(wanted_all, COL, axis=1, tiled=True)  35.4 us
    all_to_all x3, blocking collectives, sent_to_all(): return lax.all_to_all(copies, axis, split_axis=0, concat_axis=0, tiled=True)  18.6 us
    all_to_all x3, blocking collectives, summed_on_arrival(): parts = lax.all_to_all(split_up(shard, dim, count), axis, 0, 0, tiled=True)  16.6 us
  transfers between devices with their start and end apart: 6, of which 5 were waited for; matrix products, arithmetic and copies ran while one was open for 2% of the time, Pallas kernels for 0%

commit v1 on v0

--- a/solution.py
+++ b/solution.py
@@ -77,7 +77,9 @@
     unit = lax.axis_index("grp")
     gathered = lax.all_gather(activations[0], "row", axis=1, tiled=True)
     wanted_all = targets[0]
-    wanted_all = lax.all_gather(wanted_all, COL, axis=1, tiled=True)
+    wanted_all = jnp.concatenate(
+        lax.all_to_all(jnp.stack([wanted_all] * lax.axis_size(COL)), COL, 0, 0), axis=1
+    )
     first = first_moment[0]
     second = second_moment[0]
     params = outer_params

time: 410 us -> 483 us (1.18)
  starting transfers between devices: 35.7 us -> 74.2 us
  blocking collectives: 117 us -> 145 us
  local copies, waits for them, and re-layouts: 26.5 us -> 33.2 us
    all_to_all x0 -> x1, waiting for transfers between devices: none -> 41.5 us  [local(): lax.all_to_all(jnp.stack([wanted_all] * lax.axis_size(COL)), COL, 0, 0)]
    all_gather x1 -> x0, waiting for transfers between devices: 35.4 us -> none  [local(): wanted_all = lax.all_gather(wanted_all, COL, axis=1, tiled=True)]
    all_to_all x4, starting transfers between devices: 35.6 us -> 67.8 us  [sent_to_all(): return lax.all_to_all(copies, axis, split_axis=0, concat_axis=0, tiled=True)]
    all_to_all x3, blocking collectives: 18.6 us -> 40.9 us  [sent_to_all(): return lax.all_to_all(copies, axis, split_axis=0, concat_axis=0, tiled=True)]
    all_to_all x4, waiting for transfers between devices: 91.7 us -> 83.8 us  [sent_to_all(): return lax.all_to_all(copies, axis, split_axis=0, concat_axis=0, tiled=True)]
    all_to_all x0 -> x1, starting transfers between devices: none -> 6.3 us  [local(): lax.all_to_all(jnp.stack([wanted_all] * lax.axis_size(COL)), COL, 0, 0)]
    all_to_all x3, blocking collectives: 81.9 us -> 87.2 us  [sum_in_two_steps(): return jnp.sum(lax.all_to_all(own, far, 0, 0, tiled=True), axis=0)]
    unnamed x58 -> x54, local copies, waits for them, and re-layouts: 7.66 us -> 12.3 us
  transfers between devices with their start and end apart: 6 -> 6, of which waited for: 5 -> 6; matrix products, arithmetic and copies ran while one was open for 2% -> 2% of each run, Pallas kernels for 0% -> 0%
where the time goes in v1:
time: 483 us; the launch traced here: 482 us
  waiting for transfers between devices  200 us (41%)
  blocking collectives  145 us (30%)
  starting transfers between devices  74.2 us (15%)
  local copies, waits for them, and re-layouts  33.2 us (7%)
  between operations  14.5 us (3%)
  matrix products  10.9 us (2%)
    all_to_all x3, blocking collectives, sum_in_two_steps(): return jnp.sum(lax.all_to_all(own, far, 0, 0, tiled=True), axis=0)  87.2 us
    all_to_all x4, waiting for transfers between devices, sent_to_all(): return lax.all_to_all(copies, axis, split_axis=0, concat_axis=0, tiled=True)  83.8 us
    all_gather x1, waiting for transfers between devices, local(): gathered = lax.all_gather(activations[0], 'row', axis=1, tiled=True)  73.9 us
    all_to_all x4, starting transfers between devices, sent_to_all(): return lax.all_to_all(copies, axis, split_axis=0, concat_axis=0, tiled=True)  67.8 us
    all_to_all x1, waiting for transfers between devices, local(): lax.all_to_all(jnp.stack([wanted_all] * lax.axis_size(COL)), COL, 0, 0)  41.5 us
    all_to_all x3, blocking collectives, sent_to_all(): return lax.all_to_all(copies, axis, split_axis=0, concat_axis=0, tiled=True)  40.9 us
    all_to_all x3, blocking collectives, summed_on_arrival(): parts = lax.all_to_all(split_up(shard, dim, count), axis, 0, 0, tiled=True)  16.6 us
    unnamed x54, local copies, waits for them, and re-layouts  12.3 us
  transfers between devices with their start and end apart: 6, of which 6 were waited for; matrix products, arithmetic and copies ran while one was open for 2% of the time, Pallas kernels for 0%

profile of v1, /device:TPU:1, one launch (start us, length us, event | category | flops | bytes accessed | tf_op | source)
XLA Modules:
  0.0 481.5 jit_solution(14510557006877656897)
XLA Ops:
  7.9 73.9 %all-gather.3.cloned.1.call-done = bf16[1,3,2048,512]{3,2,1,0:T(8,128)(2,1)} async-done(((bf16[1,3,512,512]{3,2,1,0:T(8,128)(2,1)}), bf16[1,3,2048,512]{3,2,1,0:T(8,128)(2,1)}) %all-gather.3.cloned.1.call-update) | async-done | bytes 6291472 | tf_op jit(solution)/shard_map/all_gather | solution.py:78
  81.8 1.6 slice-done.6
  84.3 5.8 %all_to_all.70 = f32[2,8,128,256]{3,2,1,0:T(8,128)S(1)} all-to-all(f32[2,8,128,256]{3,2,1,0:T(8,128)S(1)} %copy.92), channel_id=1, replica_groups=mesh['grp'=4,'row'=4,'col_0'=4,'col_1'=2,'col_2'=2] {'col_2'}, dimensions={0} | all-to-all | bytes 4194304 | tf_op jit(solution)/shard_map/all_to_all | solution.py:28
  90.3 33.6 %all_to_all.71 = f32[8,128,256]{2,1,0:T(8,128)} all-to-all(f32[8,128,256]{2,1,0:T(8,128)S(1)} %reduce_sum.63), channel_id=1, replica_groups=mesh['grp'=4,'row'=4,'col_0'=4,'col_1'=2,'col_2'=2] {'col_0','col_1'}, dimensions={0} | all-to-all | bytes 2097152 | tf_op jit(solution)/shard_map/all_to_all | solution.py:35
  123.9 2.1 stack.3
  126.0 6.3 %all-to-all-start.4 = ((bf16[16,3,128,256]{3,2,1,0:T(8,128)(2,1)}), bf16[16,3,128,256]{3,2,1,0:T(8,128)(2,1)S(1)}, u32[]{:S(2)}, u32[]{:S(2)}) async-start(bf16[16,3,128,256]{3,2,1,0:T(8,128)(2,1)} %stack.3), calls=%async_computation.4 | async-start | bytes 6291456 | tf_op jit(solution)/shard_map/all_to_all | solution.py:81
  133.6 41.5 %all-to-all-done.4 = bf16[16,3,128,256]{3,2,1,0:T(8,128)(2,1)S(1)} async-done(((bf16[16,3,128,256]{3,2,1,0:T(8,128)(2,1)}), bf16[16,3,128,256]{3,2,1,0:T(8,128)(2,1)S(1)}, u32[]{:S(2)}, u32[]{:S(2)}) %all-to-all-start.4) | async-done | bytes 3145760 | tf_op jit(solution)/shard_map/all_to_all | solution.py:81
  176.3 35.7 %all-to-all-start.2 = ((f32[8,128,256]{2,1,0:T(8,128)}), f32[8,128,256]{2,1,0:T(8,128)}, u32[]{:S(2)}, u32[]{:S(2)}) async-start(f32[8,128,256]{2,1,0:T(8,128)} %broadcast_in_dim.21), calls=%async_computation.2 | async-start | bytes 2097152 | tf_op jit(solution)/shard_map/all_to_all | solution.py:47
  212.0 2.0 copy.115
  214.0 2.0 copy.91
  216.0 2.1 copy.95
  218.3 1.7 fusion.43
  220.0 8.8 %all-to-all-done.2 = f32[8,128,256]{2,1,0:T(8,128)} async-done(((f32[8,128,256]{2,1,0:T(8,128)}), f32[8,128,256]{2,1,0:T(8,128)}, u32[]{:S(2)}, u32[]{:S(2)}) %all-to-all-start.2) | async-done | bytes 1048608 | tf_op jit(solution)/shard_map/all_to_all | solution.py:47
  228.8 1.6 broadcast_in_dim.22
  230.4 9.1 %all_to_all.72 = f32[2,8,128,256]{3,2,1,0:T(8,128)S(1)} all-to-all(f32[2,8,128,256]{3,2,1,0:T(8,128)S(1)} %broadcast_in_dim.22), channel_id=1, replica_groups=mesh['grp'=4,'row'=4,'col_0'=4,'col_1'=2,'col_2'=2] {'col_2'}, dimensions={0} | all-to-all | bytes 4194304 | tf_op jit(solution)/shard_map/all_to_all | solution.py:47
  241.5 2.4 convolution_bitcast_fusion.1
  243.9 3.0 reshape_reshape.4
  247.1 5.4 %all_to_all.73 = f32[2,8,128,256]{2,1,3,0:T(8,128)S(1)} all-to-all(f32[2,8,128,256]{2,1,3,0:T(8,128)S(1)} %bitcast.153), channel_id=1, replica_groups=mesh['grp'=4,'row'=4,'col_0'=4,'col_1'=2,'col_2'=2] {'col_2'}, dimensions={0} | all-to-all | bytes 4194304 | tf_op jit(solution)/shard_map/all_to_all | solution.py:28
  253.0 30.9 %all_to_all.74 = f32[8,128,256]{1,2,0:T(8,128)S(1)} all-to-all(f32[8,128,256]{1,2,0:T(8,128)S(1)} %copy.100), channel_id=1, replica_groups=mesh['grp'=4,'row'=4,'col_0'=4,'col_1'=2,'col_2'=2] {'col_0','col_1'}, dimensions={0} | all-to-all | bytes 2097152 | tf_op jit(solution)/shard_map/all_to_all | solution.py:35
  285.1 3.6 all-to-all-start.7
  288.6 14.2 %all-to-all-done.7 = f32[8,128,256]{2,1,0:T(8,128)S(1)} async-done(((f32[8,128,256]{2,1,0:T(8,128)}), f32[8,128,256]{2,1,0:T(8,128)S(1)}, u32[]{:S(2)}, u32[]{:S(2)}) %all-to-all-start.7) | async-done | bytes 1048608 | tf_op jit(solution)/shard_map/all_to_all | solution.py:47
  303.1 16.8 %all_to_all.75 = f32[2,8,128,256]{3,2,1,0:T(8,128)S(1)} all-to-all(f32[2,8,128,256]{3,2,1,0:T(8,128)S(1)} %broadcast_in_dim.24), channel_id=1, replica_groups=mesh['grp'=4,'row'=4,'col_0'=4,'col_1'=2,'col_2'=2] {'col_2'}, dimensions={0} | all-to-all | bytes 4194304 | tf_op jit(solution)/shard_map/all_to_all | solution.py:47
  321.8 2.9 convolution_bitcast_fusion
  324.7 3.0 reshape_reshape.5
  327.8 5.4 %all_to_all.76 = f32[2,8,128,256]{2,1,3,0:T(8,128)S(1)} all-to-all(f32[2,8,128,256]{2,1,3,0:T(8,128)S(1)} %bitcast.154), channel_id=1, replica_groups=mesh['grp'=4,'row'=4,'col_0'=4,'col_1'=2,'col_2'=2] {'col_2'}, dimensions={0} | all-to-all | bytes 4194304 | tf_op jit(solution)/shard_map/all_to_all | solution.py:28
  333.7 22.7 %all_to_all.77 = f32[8,128,256]{1,2,0:T(8,128)S(1)} all-to-all(f32[8,128,256]{1,2,0:T(8,128)S(1)} %copy.106), channel_id=1, replica_groups=mesh['grp'=4,'row'=4,'col_0'=4,'col_1'=2,'col_2'=2] {'col_0','col_1'}, dimensions={0} | all-to-all | bytes 2097152 | tf_op jit(solution)/shard_map/all_to_all | solution.py:35
  357.6 3.7 all-to-all-start.11
  361.4 14.3 %all-to-all-done.11 = f32[8,128,256]{2,1,0:T(8,128)S(1)} async-done(((f32[8,128,256]{2,1,0:T(8,128)}), f32[8,128,256]{2,1,0:T(8,128)S(1)}, u32[]{:S(2)}, u32[]{:S(2)}) %all-to-all-start.11) | async-done | bytes 1048608 | tf_op jit(solution)/shard_map/all_to_all | solution.py:47
  375.9 15.0 %all_to_all.78 = f32[2,8,128,256]{3,2,1,0:T(8,128)S(1)} all-to-all(f32[2,8,128,256]{3,2,1,0:T(8,128)S(1)} %broadcast_in_dim.26), channel_id=1, replica_groups=mesh['grp'=4,'row'=4,'col_0'=4,'col_1'=2,'col_2'=2] {'col_2'}, dimensions={0} | all-to-all | bytes 4194304 | tf_op jit(solution)/shard_map/all_to_all | solution.py:47
  392.6 3.4 fusion.8
  397.8 24.8 %all-to-all-start.13 = ((f32[4,512,256]{2,1,0:T(8,128)}), f32[4,512,256]{2,1,0:T(8,128)S(1)}, u32[]{:S(2)}, u32[]{:S(2)}) async-start(f32[4,512,256]{2,1,0:T(8,128)} %broadcast_in_dim.27), calls=%async_computation.13 | async-start | bytes 4194304 | tf_op jit(solution)/shard_map/all_to_all | solution.py:47
  423.8 46.5 %all-to-all-done.13 = f32[4,512,256]{2,1,0:T(8,128)S(1)} async-done(((f32[4,512,256]{2,1,0:T(8,128)}), f32[4,512,256]{2,1,0:T(8,128)S(1)}, u32[]{:S(2)}, u32[]{:S(2)}) %all-to-all-start.13) | async-done | bytes 2097184 | tf_op jit(solution)/shard_map/all_to_all | solution.py:47
  (87 shorter events, 21.2 us)
Async XLA Ops:
  7.2 74.7 %all-gather.3.cloned.1.call-start = ((), (), s32[]{:S(2)}) async-start(), calls=%async_computation.14 | async-start | bytes 7864320 | tf_op jit(solution)/shard_map/all_gather | solution.py:78
  7.9 73.9 %copy-start.2 = (f32[512,256]{1,0:T(8,128)S(1)}, f32[512,256]{1,0:T(8,128)}, u32[]{:S(2)}) copy-start(f32[512,256]{1,0:T(8,128)} %param.6) | copy-start | bytes 1572868
  81.8 1.6 slice-start.6
  90.1 33.8 %copy-start.12 = (bf16[1,3,128,256]{3,2,1,0:T(8,128)(2,1)S(1)}, bf16[1,3,128,256]{3,2,1,0:T(8,128)(2,1)}, u32[]{:S(2)}) copy-start(bf16[1,3,128,256]{3,2,1,0:T(8,128)(2,1)} %param.11) | copy-start | bytes 589828
  126.0 49.1 %all-to-all-start.4 = ((bf16[16,3,128,256]{3,2,1,0:T(8,128)(2,1)}), bf16[16,3,128,256]{3,2,1,0:T(8,128)(2,1)S(1)}, u32[]{:S(2)}, u32[]{:S(2)}) async-start(bf16[16,3,128,256]{3,2,1,0:T(8,128)(2,1)} %stack.3), calls=%async_computation.4 | async-start | bytes 6291456 | tf_op jit(solution)/shard_map/all_to_all | solution.py:81
  176.3 52.6 %all-to-all-start.2 = ((f32[8,128,256]{2,1,0:T(8,128)}), f32[8,128,256]{2,1,0:T(8,128)}, u32[]{:S(2)}, u32[]{:S(2)}) async-start(f32[8,128,256]{2,1,0:T(8,128)} %broadcast_in_dim.21), calls=%async_computation.2 | async-start | bytes 2097152 | tf_op jit(solution)/shard_map/all_to_all | solution.py:47
  228.8 11.1 %slice-start = ((s8[6291456]{0:T(1024)(128)(4,1)}), s8[4194304]{0:T(1024)(128)(4,1)S(1)}, s32[]{:S(2)}) async-start(s8[6291456]{0:T(1024)(128)(4,1)} %bitcast.155), calls=%async_computation.15 | async-start | bytes 8388608
  230.4 9.5 %slice-start.1 = ((s8[6291456]{0:T(1024)(128)(4,1)}), s8[2097152]{0:T(1024)(128)(4,1)S(1)}, s32[]{:S(2)}) async-start(s8[6291456]{0:T(1024)(128)(4,1)} %bitcast.155), calls=%async_computation.16 | async-start | bytes 4194304
  239.9 1.6 copy-start.3
  240.0 1.6 copy-start.6
  240.0 1.5 copy-start.9
  240.7 0.8 copy-start.13
  285.1 17.8 %all-to-all-start.7 = ((f32[8,128,256]{2,1,0:T(8,128)}), f32[8,128,256]{2,1,0:T(8,128)S(1)}, u32[]{:S(2)}, u32[]{:S(2)}) async-start(f32[8,128,256]{2,1,0:T(8,128)} %broadcast_in_dim.23), calls=%async_computation.7 | async-start | bytes 2097152 | tf_op jit(solution)/shard_map/all_to_all | solution.py:47
  302.8 17.4 %slice-start.2 = ((s8[6291456]{0:T(1024)(128)(4,1)}), s8[4194304]{0:T(1024)(128)(4,1)S(1)}, s32[]{:S(2)}) async-start(s8[6291456]{0:T(1024)(128)(4,1)} %bitcast.157), calls=%async_computation.17 | async-start | bytes 8388608
  303.0 16.8 %copy-start.1 = (bf16[1,16,128,256]{3,2,1,0:T(8,128)(2,1)S(1)}, bf16[1,16,128,256]{3,2,1,0:T(8,128)(2,1)}, u32[]{:S(2)}) copy-start(bf16[1,16,128,256]{3,2,1,0:T(8,128)(2,1)} %get-tuple-element.16) | copy-start | bytes 3145732
  303.0 17.1 %slice-start.3 = ((s8[6291456]{0:T(1024)(128)(4,1)}), s8[2097152]{0:T(1024)(128)(4,1)S(1)}, s32[]{:S(2)}) async-start(s8[6291456]{0:T(1024)(128)(4,1)} %bitcast.157), calls=%async_computation.18 | async-start | bytes 4194304
  320.2 1.6 copy-start.4
  320.2 1.6 copy-start.7
  320.2 1.6 copy-start.10
  320.2 1.5 copy-start.14
  321.0 0.8 copy-start.16
  357.6 18.0 %all-to-all-start.11 = ((f32[8,128,256]{2,1,0:T(8,128)}), f32[8,128,256]{2,1,0:T(8,128)S(1)}, u32[]{:S(2)}, u32[]{:S(2)}) async-start(f32[8,128,256]{2,1,0:T(8,128)} %broadcast_in_dim.25), calls=%async_computation.11 | async-start | bytes 2097152 | tf_op jit(solution)/shard_map/all_to_all | solution.py:47
  375.7 15.6 %slice-start.4 = ((s8[6291456]{0:T(1024)(128)(4,1)}), s8[4194304]{0:T(1024)(128)(4,1)S(1)}, s32[]{:S(2)}) async-start(s8[6291456]{0:T(1024)(128)(4,1)} %bitcast.159), calls=%async_computation.19 | async-start | bytes 8388608
  375.9 15.1 %copy-start = (bf16[1,16,128,256]{3,2,1,0:T(8,128)(2,1)S(1)}, bf16[1,16,128,256]{3,2,1,0:T(8,128)(2,1)}, u32[]{:S(2)}) copy-start(bf16[1,16,128,256]{3,2,1,0:T(8,128)(2,1)} %get-tuple-element.15) | copy-start | bytes 3145732
  375.9 15.4 %slice-start.5 = ((s8[6291456]{0:T(1024)(128)(4,1)}), s8[2097152]{0:T(1024)(128)(4,1)S(1)}, s32[]{:S(2)}) async-start(s8[6291456]{0:T(1024)(128)(4,1)} %bitcast.159), calls=%async_computation.20 | async-start | bytes 4194304
  391.0 1.0 copy-start.5
  391.0 1.2 copy-start.8
  391.0 1.4 copy-start.11
  391.0 1.5 copy-start.15
  391.0 1.7 copy-start.17
  397.8 72.6 %all-to-all-start.13 = ((f32[4,512,256]{2,1,0:T(8,128)}), f32[4,512,256]{2,1,0:T(8,128)S(1)}, u32[]{:S(2)}, u32[]{:S(2)}) async-start(f32[4,512,256]{2,1,0:T(8,128)} %broadcast_in_dim.27), calls=%async_computation.13 | async-start | bytes 4194304 | tf_op jit(solution)/shard_map/all_to_all | solution.py:47
Sparse Core Ops, SparseCore 0:
  9.8 71.9 all-gather.2
